TPU v7x, 128 devices: a whole 4x4x4 slice. The times are simulated.
128 devices in a mesh: slab: 16 (over x_hi, z, core), col: 8 (over x_lo, y).
Axes of the slice: x: 4 (x_hi: 2, x_lo: 2; x = x_hi * 2 + x_lo), y: 4, z: 4, core: 2. Of those that a mesh axis runs over, the one named last changes fastest.
Arguments:
- sensitivity: bfloat16 [3, 512, 65536], P(None, 'col', 'slab'), may hold values from -0.03125 to 0.03125
- residual_force: bfloat16 [3, 65536], P(None, 'slab'), may hold values from -6 to 6
- moments: float32 [6, 64, 1024], P(None, 'slab'), as said below
- zone_label: int32 [64, 1024], P('slab'), may hold values from 0 to 511, as said below
- misfit: float32 [64, 1024], P('slab'), may hold values from 0.1 to 10
Outputs:
- hessian: float32 [512, 512], P('col', 'slab')
- gradient: float32 [512], replicated
- zone_misfit: float32 [512], replicated
Inputs may be any that keep to these rules, and one draw needn't show every extreme that they name: zone_label is the box of a 8 x 8 x 8 partition of the specimen that holds the element, the in-plane box borders displaced by at most one element; every zone occurs. `moments`: each element's moment matrix is symmetric with positive diagonal, and each diagonal entry exceeds the sum of the magnitudes of the others in its row.
All inputs are finite; a program needn't handle non-finite values.
Results may differ from a plain program's by a relative error of at most 0.0003.
Values may be sent and summed in bfloat16 or wider, within the bound.
A program may use at most 128 MiB of HBM per device.

v0:
```python
import jax
import jax.numpy as jnp
from jax import lax
from jax.sharding import PartitionSpec as P

GX = 64
GY = 16
third = 1.0 / 3.0
sixth = 1.0 / 6.0


def shifted(value, axis, by):
    count = lax.axis_size(axis)
    pairs = [(i, i + by) for i in range(count) if 0 <= i + by < count]
    return lax.ppermute(value, axis, pairs)


def mix_pair(first, second):
    return (third * first + sixth * second, sixth * first + third * second)


def shift_ahead(field, step, keep):
    moved = jnp.concatenate([field[..., step:], jnp.zeros_like(field[..., :step])], axis=-1)
    if keep is None:
        return moved
    return jnp.where(keep, moved, 0.0)


def shift_behind(field, step, keep):
    moved = jnp.concatenate([jnp.zeros_like(field[..., :step]), field[..., :-step]], axis=-1)
    if keep is None:
        return moved
    return jnp.where(keep, moved, 0.0)


def apply_moments(moments, field):
    comps = [moments[k][None, :] for k in range(6)]
    first, second, last = (field[0], field[1], field[2])
    out_x = comps[0] * first + comps[3] * second + comps[4] * last
    out_y = comps[3] * first + comps[1] * second + comps[5] * last
    out_z = comps[4] * first + comps[5] * second + comps[2] * last
    return jnp.stack([out_x, out_y, out_z])


def element_layer(lower, upper, moments):
    plane = lower.shape[-1]
    pos_y = jnp.arange(plane, dtype=jnp.int32) % GY
    not_last = pos_y != GY - 1
    not_first = pos_y != 0
    mixed_z = mix_pair(lower, upper)
    results = []
    for side_z in range(2):
        field = mixed_z[side_z]
        mixed_x = mix_pair(field, shift_ahead(field, GY, None))
        values = []
        for side_x in range(2):
            layer = mixed_x[side_x]
            mixed_y = mix_pair(layer, shift_ahead(layer, 1, not_last))
            values.append([apply_moments(moments, mixed_y[side_y]) for side_y in range(2)])
        total = values[0][0]
        total = total + shift_behind(values[1][0], GY, None)
        total = total + shift_behind(values[0][1], 1, not_first)
        total = total + shift_behind(shift_behind(values[1][1], 1, not_first), GY, None)
        results.append(total)
    return (results[0], results[1])


def on_device(sensitivity, residual_force, moments, zone_label, misfit):
    cols = sensitivity.shape[1]
    layers = moments.shape[1]
    plane_size = GX * GY
    n_slab = lax.axis_size("slab")
    n_col = lax.axis_size("col")
    width = cols * n_col
    field = sensitivity.reshape(3, cols, layers, plane_size)
    above = shifted(sensitivity[:, :, :plane_size], "slab", -1)
    levels = []
    carry = None
    first_lower = None
    for level in range(layers):
        lower = field[:, :, level].astype(jnp.float32)
        if level + 1 < layers:
            upper = field[:, :, level + 1].astype(jnp.float32)
        else:
            upper = above.astype(jnp.float32)
        to_lower, to_upper = element_layer(lower, upper, moments[:, level])
        if level == 0:
            first_lower = to_lower
        else:
            levels.append((carry + to_lower).astype(jnp.bfloat16))
        carry = to_upper
    from_below = shifted(carry.astype(jnp.bfloat16), "slab", 1).astype(carry.dtype)
    levels.insert(0, (from_below + first_lower).astype(jnp.bfloat16))
    image = jnp.stack(levels, axis=2).reshape(3, cols, layers * plane_size)
    panel_rows = lax.dot_general(
        image,
        lax.all_gather(sensitivity, "col", axis=1, tiled=True),
        (((0, 2), (0, 2)), ((), ())),
        preferred_element_type=jnp.float32,
    )
    hessian = lax.psum_scatter(panel_rows, "slab", scatter_dimension=1, tiled=True)
    grad_part = lax.dot_general(
        residual_force,
        sensitivity,
        (((0, 1), (0, 2)), ((), ())),
        preferred_element_type=jnp.float32,
    )
    grad_full = lax.dynamic_update_slice_in_dim(
        jnp.zeros((width,), jnp.float32), grad_part, lax.axis_index("col") * cols, 0
    )
    elements = layers * plane_size
    share = elements // n_col
    offset = lax.axis_index("col") * share
    zone_part = lax.dynamic_slice_in_dim(zone_label.reshape(elements), offset, share, 0)
    misfit_part = lax.dynamic_slice_in_dim(misfit.reshape(elements), offset, share, 0)
    onehot = (zone_part[:, None] == jnp.arange(width, dtype=jnp.int32)[None, :]).astype(jnp.float32)
    zone_part_sum = jnp.dot(misfit_part, onehot, precision=lax.Precision.HIGHEST)
    gradient, zone_sums = lax.psum((grad_full, zone_part_sum), ("slab", "col"))
    zone_misfit = zone_sums * (width / (elements * n_slab))
    return (hessian, gradient, zone_misfit)


def solution(mesh):
    in_specs = (
        P(None, "col", "slab"),
        P(None, "slab"),
        P(None, "slab", None),
        P("slab", None),
        P("slab", None),
    )
    out_specs = (P("col", "slab"), P(), P())
    return jax.shard_map(
        on_device, mesh=mesh, in_specs=in_specs, out_specs=out_specs, check_vma=False
    )
```

profile of v0, /device:TPU:0, one launch (start us, length us, event | category | flops | bytes accessed | tf_op | source)
XLA Modules:
  0.0 330.2 jit_solution(12702796365399645540)
XLA Ops:
  8.6 0.8 slice.768
  9.3 1.3 collective-permute-start
  10.6 1.2 reshape.1815
  11.8 3.2 fusion.94
  15.0 0.9 copy-done.1
  16.3 0.9 copy-done.3
  17.2 1.2 slice.966
  19.5 1.4 fusion.96
  21.0 1.2 fusion.14
  22.2 1.3 multiply_add_fusion.41
  24.0 1.4 slice.1015
  25.4 2.3 slice.999
  27.7 1.2 slice.967
  28.9 1.2 slice.971
  30.2 161.3 %all-reduce.56 = (f32[512]{0:T(512)}, f32[512]{0:T(512)}) all-reduce(f32[512]{0:T(512)S(1)} %dynamic_update_slice.3, f32[512]{0:T(512)S(1)} %bitcast.370), channel_id=1, replica_groups=mesh['slab'=16,'col'=8] {'slab','col'}, use_global_device_ids=true, to_apply=%region_1.2 | all-reduce | flops 1024 | bytes 8192 | tf_op jit(solution)/shard_map/psum | solution.py:118
  192.8 1.5 fusion.3
  194.6 1.2 fusion.5
  196.2 2.6 multiply_add_fusion.45
  199.9 1.2 slice.1048
  201.1 1.2 slice.1052
  202.3 1.2 slice.1064
  203.4 1.1 slice.1068
  204.6 1.2 slice.953
  206.4 1.1 slice.983
  207.6 1.2 slice.987
  208.7 1.2 slice.1000
  209.9 1.2 slice.949
  211.1 1.2 slice.1004
  212.2 1.2 slice.1016
  213.4 1.2 slice.1020
  214.6 1.1 slice.1032
  215.7 1.2 slice.1036
  216.9 5.2 %multiply_add_fusion.42 = (f32[3,64,1024]{2,1,0:T(8,128)}, f32[3,64,1024]{2,1,0:T(8,128)}, f32[3,64,1024]{2,1,0:T(8,128)S(1)}, f32[3,64,1024]{2,1,0:T(8,128)S(1)...) fusion(f32[3,64,1024]{2,1,0:T(8,128)S(1)} %get-tuple-element.43, ...), kind=kLoop, calls=%fused_computation.212 | loop fusion | flops 8257536 | bytes 18870784 | tf_op jit(solution)/shard_map/add | solution.py:19
  222.1 2.1 multiply_add_fusion.122
  224.2 0.9 multiply_add_fusion.110
  225.2 5.7 %multiply_add_fusion.46 = (f32[3,64,1024]{2,1,0:T(8,128)}, f32[3,64,1024]{2,1,0:T(8,128)}, f32[3,64,1024]{2,1,0:T(8,128)}, f32[3,64,1024]{2,1,0:T(8,128)S(1)}, f...) fusion(f32[3,64,1024]{2,1,0:T(8,128)S(1)} %get-tuple-element.44, ...), kind=kLoop, calls=%fused_computation.217 | loop fusion | flops 8257536 | bytes 18870784 | tf_op jit(solution)/shard_map/add | solution.py:19
  231.0 1.3 multiply_add_fusion.98
  232.7 0.8 copy-done.10
  234.0 0.7 copy-done.9
  236.0 1.5 fusion.76
  238.3 1.8 collective-permute-start.1
  240.2 1.0 multiply_add_fusion.10
  242.4 0.8 copy-done.5
  245.9 1.4 fusion.87
  247.3 1.3 fusion.86
  248.6 1.3 fusion.85
  251.0 7.1 %convolution_bitcast_fusion = f32[64,512]{0,1:T(8,128)} fusion(bf16[3,64,4096]{2,1,0:T(8,128)(2,1)S(1)} %bitcast.171, bf16[3,512,4096]{2,1,0:T(8,128)(2,1)} %all-gather.2.cloned.1.call-done), kind=kOutput, calls=%fused_computation.1 | convolution fusion | flops 805306368 | bytes 14286848 | tf_op jit(solution)/shard_map/dot_general | solution.py:95
  258.7 64.7 %reduce-scatter.2.cloned.1.call-done = f32[64,32]{0,1:T(8,128)} async-done(((f32[64,512]{0,1:T(8,128)}), f32[64,32]{0,1:T(8,128)}) %reduce-scatter.2.cloned.1.call-update) | async-done | bytes 8208 | tf_op jit(solution)/shard_map/reduce_scatter | solution.py:101
  (160 shorter events, 15.4 us)
Async XLA Ops:
  7.2 1.4 copy-start
  7.2 243.8 %all-gather.2.cloned.1.call-start = ((), (), s32[]{:S(2)}) async-start(), calls=%async_computation.1 | async-start | bytes 14155776 | tf_op jit(solution)/shard_map/all_gather | solution.py:97
  7.9 315.5 %reduce-scatter.2.cloned.1.call-start = ((), (), s32[]{:S(2)}) async-start(), calls=%async_computation.2 | async-start | bytes 278528 | tf_op jit(solution)/shard_map/reduce_scatter | solution.py:101
  9.3 183.5 %collective-permute-start = (bf16[3,64,1024]{2,1,0:T(8,128)(2,1)}, bf16[3,64,1024]{2,1,0:T(8,128)(2,1)}, u32[]{:S(2)}, u32[]{:S(2)}) collective-permute-start(bf16[3,64,1024]{2,1,0:T(8,128)(2,1)} %slice.768), channel_id=1, source_target_pairs={{8,0},{16,8},{24,16},{32,24},{40,32},{48,40},{56,48},{64,56},{72,6... | collective-permute-start | bytes 1179656 | tf_op jit(solution)/shard_map/ppermute | solution.py:15
  15.9 2.4 copy-start.47
  15.9 2.4 copy-start.48
  15.9 2.6 copy-start.51
  17.2 3.8 %copy-start.19 = (bf16[3,64,1,1024]{3,2,1,0:T(2,128)(2,1)S(1)}, bf16[3,64,1,1024]{3,2,1,0:T(2,128)(2,1)}, u32[]{:S(2)}) copy-start(bf16[3,64,1,1024]{3,2,1,0:T(2,128)(2,1)} %get-tuple-element.57) | copy-start | bytes 1179652
  19.1 3.1 copy-start.4
  19.1 3.1 copy-start.18
  27.7 164.5 %copy-start.45 = (f32[6,4,1024]{2,1,0:T(4,128)S(1)}, f32[6,4,1024]{2,1,0:T(4,128)}, u32[]{:S(2)}) copy-start(f32[6,4,1024]{2,1,0:T(4,128)} %param.7) | copy-start | bytes 294916
  194.6 1.5 copy-start.2
  194.6 1.5 copy-start.17
  214.6 2.3 copy-start.49
  216.9 5.2 %copy-start.25 = (f32[1,1,1024]{2,1,0:T(1,128)S(1)}, f32[1,1,1024]{2,1,0:T(1,128)}, u32[]{:S(2)}) copy-start(f32[1,1,1024]{2,1,0:T(1,128)} %get-tuple-element.188) | copy-start | bytes 12292
  216.9 5.2 %copy-start.26 = (f32[1,1,1024]{2,1,0:T(1,128)S(1)}, f32[1,1,1024]{2,1,0:T(1,128)}, u32[]{:S(2)}) copy-start(f32[1,1,1024]{2,1,0:T(1,128)} %get-tuple-element.189) | copy-start | bytes 12292
  222.1 2.1 copy-start.11
  225.2 5.7 %copy-start.29 = (f32[1,1,1024]{2,1,0:T(1,128)S(1)}, f32[1,1,1024]{2,1,0:T(1,128)}, u32[]{:S(2)}) copy-start(f32[1,1,1024]{2,1,0:T(1,128)} %get-tuple-element.179) | copy-start | bytes 12292
  225.2 5.7 %copy-start.30 = (f32[1,1,1024]{2,1,0:T(1,128)S(1)}, f32[1,1,1024]{2,1,0:T(1,128)}, u32[]{:S(2)}) copy-start(f32[1,1,1024]{2,1,0:T(1,128)} %get-tuple-element.180) | copy-start | bytes 12292
  225.2 5.7 %copy-start.31 = (f32[1,1,1024]{2,1,0:T(1,128)S(1)}, f32[1,1,1024]{2,1,0:T(1,128)}, u32[]{:S(2)}) copy-start(f32[1,1,1024]{2,1,0:T(1,128)} %get-tuple-element.181) | copy-start | bytes 12292
  225.2 5.7 %copy-start.32 = (f32[1,1,1024]{2,1,0:T(1,128)S(1)}, f32[1,1,1024]{2,1,0:T(1,128)}, u32[]{:S(2)}) copy-start(f32[1,1,1024]{2,1,0:T(1,128)} %get-tuple-element.182) | copy-start | bytes 12292
  225.2 5.7 %copy-start.33 = (f32[1,1,1024]{2,1,0:T(1,128)S(1)}, f32[1,1,1024]{2,1,0:T(1,128)}, u32[]{:S(2)}) copy-start(f32[1,1,1024]{2,1,0:T(1,128)} %get-tuple-element.183) | copy-start | bytes 12292
  225.2 5.7 %copy-start.34 = (f32[1,1,1024]{2,1,0:T(1,128)S(1)}, f32[1,1,1024]{2,1,0:T(1,128)}, u32[]{:S(2)}) copy-start(f32[1,1,1024]{2,1,0:T(1,128)} %get-tuple-element.184) | copy-start | bytes 12292
  230.9 1.5 copy-start.12
  230.9 1.6 copy-start.7
  230.9 1.6 copy-start.35
  231.0 1.6 copy-start.36
  231.0 1.6 copy-start.37
  231.0 1.6 copy-start.42
  231.0 1.6 copy-start.43
  231.0 1.6 copy-start.44
  232.6 1.2 copy-start.6
  233.5 1.2 copy-start.9
  233.8 1.2 copy-start.8
  233.8 1.2 copy-start.27
  233.8 1.2 copy-start.28
  233.8 1.2 copy-start.38
  233.8 1.2 copy-start.39
  233.8 1.2 copy-start.40
  234.7 1.2 copy-start.23
  234.7 1.3 copy-start.24
  234.7 1.3 copy-start.46
  237.6 2.6 copy-start.13
  237.6 2.6 copy-start.14
  237.6 2.6 copy-start.15
  237.6 2.6 copy-start.16
  238.3 11.5 %collective-permute-start.1 = (bf16[3,64,1024]{2,1,0:T(8,128)(2,1)S(1)}, bf16[3,64,1024]{2,1,0:T(8,128)(2,1)S(1)}, u32[]{:S(2)}, u32[]{:S(2)}) collective-permute-start(bf16[3,64,1024]{2,1,0:T(8,128)(2,1)S(1)} %fusion.81), channel_id=1, source_target_pairs={{0,8},{8,16},{16,24},{24,32},{32,40},{40,48},{48,56},{56,64},{64,7... | collective-permute-start | bytes 1179656 | tf_op jit(solution)/shard_map/ppermute | solution.py:15
  251.0 7.1 %copy-start.50 = (f32[512]{0:T(512)S(1)}, f32[512]{0:T(512)}, u32[]{:S(2)}) copy-start(f32[512]{0:T(512)} %get-tuple-element.4) | copy-start | bytes 6148
  (8 other events, 8.5 us)
Sparse Core Ops, SparseCore 0:
  9.6 134.1 all-gather.1
  258.2 65.1 reduce-scatter.1
where the time goes:
time: 331 us; the launch traced here: 330 us
  blocking collectives  161 us (49%)
  waiting for transfers between devices  65.4 us (20%)
  other arithmetic  38.8 us (12%)
  local copies, waits for them, and re-layouts  38.6 us (12%)
  between operations  14.8 us (4%)
  matrix products  8.09 us (2%)
    psum x1, blocking collectives, on_device(): gradient, zone_sums = lax.psum((grad_full, zone_part_sum), ('slab', 'col'))  161 us
    reduce_scatter x1, waiting for transfers between devices, on_device(): lax.psum_scatter(panel_rows, 'slab', scatter_dimension=1, tiled=True)  64.7 us
    slice x24, local copies, waits for them, and re-layouts, shift_ahead(): field[..., step:]  24.9 us
    add x11, other arithmetic, mix_pair(): return (third * first + sixth * second, sixth * first + third * second)  21 us
    add x32, other arithmetic, apply_moments(): out_x = comps[0] * first + comps[3] * second + comps[4] * last  8.5 us
    dot_general x1, matrix products, on_device(): lax.dot_general(image, lax.all_gather(sensitivity, 'col', axis=1, tiled=T...  7.08 us
  transfers between devices with their start and end apart: 4, of which 1 were waited for; matrix products, arithmetic and copies ran while one was open for 22% of the time, Pallas kernels for 0%

commit v1 on v0

--- a/solution.py
+++ b/solution.py
@@ -66,6 +66,10 @@
 
 
 def on_device(sensitivity, residual_force, moments, zone_label, misfit):
+
+    def _mix_widths(mine):
+        return lax.psum(lax.psum(mine, axis_name="slab"), axis_name="col")
+
     cols = sensitivity.shape[1]
     layers = moments.shape[1]
     plane_size = GX * GY
@@ -115,7 +119,7 @@
     misfit_part = lax.dynamic_slice_in_dim(misfit.reshape(elements), offset, share, 0)
     onehot = (zone_part[:, None] == jnp.arange(width, dtype=jnp.int32)[None, :]).astype(jnp.float32)
     zone_part_sum = jnp.dot(misfit_part, onehot, precision=lax.Precision.HIGHEST)
-    gradient, zone_sums = lax.psum((grad_full, zone_part_sum), ("slab", "col"))
+    gradient, zone_sums = _mix_widths((grad_full, zone_part_sum))
     zone_misfit = zone_sums * (width / (elements * n_slab))
     return (hessian, gradient, zone_misfit)
 

time: 331 us -> 231 us (0.70)
  blocking collectives: 161 us -> 63.2 us
    psum x1 -> x2, blocking collectives: 161 us -> 63.2 us  [_mix_widths(): return lax.psum(lax.psum(mine, axis_name='slab'), axis_name='col')]
  transfers between devices with their start and end apart: 4 -> 4, of which waited for: 1 -> 1; matrix products, arithmetic and copies ran while one was open for 22% -> 32% of each run, Pallas kernels for 0% -> 0%
where the time goes in v1:
time: 231 us; the launch traced here: 230 us
  waiting for transfers between devices  63.6 us (28%)
  blocking collectives  63.2 us (27%)
  other arithmetic  39 us (17%)
  local copies, waits for them, and re-layouts  38.7 us (17%)
  between operations  14.8 us (6%)
  matrix products  8.1 us (4%)
  starting transfers between devices  2.8 us (1%)
    psum x2, blocking collectives, _mix_widths(): return lax.psum(lax.psum(mine, axis_name='slab'), axis_name='col')  63.2 us
    reduce_scatter x1, waiting for transfers between devices, on_device(): lax.psum_scatter(panel_rows, 'slab', scatter_dimension=1, tiled=True)  62.9 us
    slice x24, local copies, waits for them, and re-layouts, shift_ahead(): field[..., step:]  25 us
    add x11, other arithmetic, mix_pair(): return (third * first + sixth * second, sixth * first + third * second)  21.2 us
    add x32, other arithmetic, apply_moments(): out_x = comps[0] * first + comps[3] * second + comps[4] * last  8.53 us
    dot_general x1, matrix products, on_device(): lax.dot_general(image, lax.all_gather(sensitivity, 'col', axis=1, tiled=T...  7.08 us
    unnamed x106, local copies, waits for them, and re-layouts  6.02 us
    another operation x4, other arithmetic, on_device(): image = jnp.stack(levels, axis=2).reshape(3, cols, layers * plane_size)  4.64 us
  transfers between devices with their start and end apart: 4, of which 1 were waited for; matrix products, arithmetic and copies ran while one was open for 32% of the time, Pallas kernels for 0%

profile of v1, /device:TPU:0, one launch (start us, length us, event | category | flops | bytes accessed | tf_op | source)
XLA Modules:
  0.0 230.2 jit_solution(7889365594550435397)
XLA Ops:
  8.6 0.8 slice.768
  9.3 1.3 collective-permute-start
  10.6 1.2 reshape.1815
  11.8 3.2 %fusion.94 = (bf16[3,64,1,1024]{3,2,1,0:T(2,128)(2,1)}, bf16[3,64,1,1024]{3,2,1,0:T(2,128)(2,1)S(1)}, bf16[3,64,1,1024]{3,2,1,0:T(2,128)(2,1)}, bf16[3,64,1,1024]{3,2,1,0:T(2,128)(2,1)S(1)}) fusion(bf16[3,64,4,1024]{3,2,1,0:T(4,128)(2,1)S(1)} %reshape.1815), kind=kLoop, calls=%fused_computation.332 | loop fusion | bytes 3145728 | tf_op jit(solution)/shard_map/slice | solution.py:87
  15.0 0.9 copy-done.1
  16.3 0.9 copy-done.3
  17.2 1.2 slice.966
  19.6 1.4 fusion.96
  21.0 1.2 fusion.14
  22.2 1.3 multiply_add_fusion.41
  24.1 1.4 slice.1015
  25.5 2.3 %slice.999 = f32[3,64,1008]{2,1,0:T(8,128)} slice(f32[3,64,1024]{2,1,0:T(8,128)} %get-tuple-element.11), slice={[0:3], [0:64], [16:1024]} | slice | bytes 1548288 | tf_op jit(solution)/shard_map/slice | solution.py:23
  27.8 1.2 slice.967
  28.9 1.2 slice.971
  30.3 43.2 %all-reduce.56 = (f32[512]{0:T(512)S(1)}, f32[512]{0:T(512)S(1)}) all-reduce(f32[512]{0:T(512)S(1)} %dynamic_update_slice.3, f32[512]{0:T(512)S(1)} %bitcast.370), channel_id=1, replica_groups=mesh['slab'=16,'col'=8] {'slab'}, use_global_device_ids=true, to_apply=%region_1.2 | all-reduce | flops 1024 | bytes 8192 | tf_op jit(solution)/shard_map/psum | solution.py:71
  73.5 20.0 %all-reduce.57 = (f32[512]{0:T(512)}, f32[512]{0:T(512)}) all-reduce(f32[512]{0:T(512)S(1)} %get-tuple-element.3, f32[512]{0:T(512)S(1)} %get-tuple-element.4), channel_id=1, replica_groups=mesh['slab'=16,'col'=8] {'col'}, use_global_device_ids=true, to_apply=%region_2.3 | all-reduce | flops 1024 | bytes 8192 | tf_op jit(solution)/shard_map/psum | solution.py:71
  94.7 1.5 fusion.3
  96.6 1.2 fusion.5
  98.1 2.6 %multiply_add_fusion.45 = (f32[3,64,1024]{2,1,0:T(8,128)S(1)}, f32[3,64,1024]{2,1,0:T(8,128)S(1)}, f32[3,64,1024]{2,1,0:T(8,128)S(1)}, f32[3,64,1024]{2,1,0:T(8,...) fusion(f32[3,64,1008]{2,1,0:T(8,128)S(1)} %slice.948, ...), kind=kLoop, calls=%fused_computation.216 | loop fusion | flops 8847360 | bytes 13713408 | tf_op jit(solution)/shard_map/add | solution.py:19
  101.9 1.2 slice.1048
  103.0 1.2 slice.1052
  104.2 1.2 slice.1064
  105.4 1.2 slice.1068
  106.6 1.2 slice.953
  108.4 1.1 slice.983
  109.5 1.2 slice.987
  110.7 1.2 slice.1000
  111.9 1.1 slice.949
  113.0 1.2 slice.1004
  114.2 1.2 slice.1016
  115.4 1.2 slice.1020
  116.5 1.2 slice.1032
  117.7 1.2 slice.1036
  118.9 5.3 %multiply_add_fusion.42 = (f32[3,64,1024]{2,1,0:T(8,128)}, f32[3,64,1024]{2,1,0:T(8,128)}, f32[3,64,1024]{2,1,0:T(8,128)S(1)}, f32[3,64,1024]{2,1,0:T(8,128)S(1)...) fusion(f32[3,64,1024]{2,1,0:T(8,128)S(1)} %get-tuple-element.45, ...), kind=kLoop, calls=%fused_computation.212 | loop fusion | flops 8257536 | bytes 18870784 | tf_op jit(solution)/shard_map/add | solution.py:19
  124.2 2.2 multiply_add_fusion.122
  126.3 0.9 multiply_add_fusion.110
  127.3 5.8 %multiply_add_fusion.46 = (f32[3,64,1024]{2,1,0:T(8,128)}, f32[3,64,1024]{2,1,0:T(8,128)}, f32[3,64,1024]{2,1,0:T(8,128)}, f32[3,64,1024]{2,1,0:T(8,128)S(1)}, f...) fusion(f32[3,64,1024]{2,1,0:T(8,128)S(1)} %get-tuple-element.46, ...), kind=kLoop, calls=%fused_computation.217 | loop fusion | flops 8257536 | bytes 18870784 | tf_op jit(solution)/shard_map/add | solution.py:19
  133.2 1.3 multiply_add_fusion.98
  134.9 0.8 copy-done.10
  138.2 1.5 fusion.76
  140.5 1.4 collective-permute-start.1
  142.0 1.0 multiply_add_fusion.10
  144.2 0.8 copy-done.5
  147.7 1.4 fusion.87
  149.1 1.3 fusion.86
  150.4 1.3 fusion.85
  152.8 7.1 %convolution_bitcast_fusion = f32[64,512]{0,1:T(8,128)} fusion(bf16[3,64,4096]{2,1,0:T(8,128)(2,1)S(1)} %bitcast.171, bf16[3,512,4096]{2,1,0:T(8,128)(2,1)} %all-gather.2.cloned.1.call-done), kind=kOutput, calls=%fused_computation.1 | convolution fusion | flops 805306368 | bytes 14286848 | tf_op jit(solution)/shard_map/dot_general | solution.py:99
  160.5 62.9 %reduce-scatter.2.cloned.1.call-done = f32[64,32]{0,1:T(8,128)} async-done(((f32[64,512]{0,1:T(8,128)}), f32[64,32]{0,1:T(8,128)}) %reduce-scatter.2.cloned.1.call-update) | async-done | bytes 8208 | tf_op jit(solution)/shard_map/reduce_scatter | solution.py:105
  (161 shorter events, 16.2 us)
Async XLA Ops:
  7.2 1.4 copy-start
  7.2 145.6 %all-gather.2.cloned.1.call-start = ((), (), s32[]{:S(2)}) async-start(), calls=%async_computation.1 | async-start | bytes 14155776 | tf_op jit(solution)/shard_map/all_gather | solution.py:101
  7.9 215.5 %reduce-scatter.2.cloned.1.call-start = ((), (), s32[]{:S(2)}) async-start(), calls=%async_computation.2 | async-start | bytes 278528 | tf_op jit(solution)/shard_map/reduce_scatter | solution.py:105
  9.3 85.4 %collective-permute-start = (bf16[3,64,1024]{2,1,0:T(8,128)(2,1)}, bf16[3,64,1024]{2,1,0:T(8,128)(2,1)}, u32[]{:S(2)}, u32[]{:S(2)}) collective-permute-start(bf16[3,64,1024]{2,1,0:T(8,128)(2,1)} %slice.768), channel_id=1, source_target_pairs={{8,0},{16,8},{24,16},{32,24},{40,32},{48,40},{56,48},{64,56},{72,6... | collective-permute-start | bytes 1179656 | tf_op jit(solution)/shard_map/ppermute | solution.py:15
  15.9 2.5 %copy-start.47 = (f32[4,1024]{1,0:T(4,128)S(1)}, f32[4,1024]{1,0:T(4,128)}, u32[]{:S(2)}) copy-start(f32[4,1024]{1,0:T(4,128)} %param.9) | copy-start | bytes 49156
  15.9 2.5 %copy-start.48 = (s32[4,1024]{1,0:T(4,128)S(1)}, s32[4,1024]{1,0:T(4,128)}, u32[]{:S(2)}) copy-start(s32[4,1024]{1,0:T(4,128)} %param.8) | copy-start | bytes 49156
  16.0 2.6 %copy-start.51 = (bf16[3,4096]{1,0:T(4,128)(2,1)S(1)}, bf16[3,4096]{1,0:T(4,128)(2,1)}, u32[]{:S(2)}) copy-start(bf16[3,4096]{1,0:T(4,128)(2,1)} %param.6) | copy-start | bytes 73732
  17.2 3.8 %copy-start.19 = (bf16[3,64,1,1024]{3,2,1,0:T(2,128)(2,1)S(1)}, bf16[3,64,1,1024]{3,2,1,0:T(2,128)(2,1)}, u32[]{:S(2)}) copy-start(bf16[3,64,1,1024]{3,2,1,0:T(2,128)(2,1)} %get-tuple-element.59) | copy-start | bytes 1179652
  19.1 3.1 %copy-start.4 = (f32[3,64,1024]{2,1,0:T(8,128)S(1)}, f32[3,64,1024]{2,1,0:T(8,128)}, u32[]{:S(2)}) copy-start(f32[3,64,1024]{2,1,0:T(8,128)} %copy-done.3) | copy-start | bytes 2359300
  19.1 3.1 %copy-start.18 = (f32[3,64,1008]{2,1,0:T(8,128)S(1)}, f32[3,64,1008]{2,1,0:T(8,128)}, u32[]{:S(2)}) copy-start(f32[3,64,1008]{2,1,0:T(8,128)} %slice.966) | copy-start | bytes 2322436
  27.8 66.3 %copy-start.45 = (f32[6,4,1024]{2,1,0:T(4,128)S(1)}, f32[6,4,1024]{2,1,0:T(4,128)}, u32[]{:S(2)}) copy-start(f32[6,4,1024]{2,1,0:T(4,128)} %param.7) | copy-start | bytes 294916
  96.5 1.5 copy-start.2
  96.6 1.5 copy-start.17
  116.5 2.3 %copy-start.49 = (pred[1024]{0:T(1024)(128)(4,1)S(1)}, pred[1024]{0:T(1024)(128)(4,1)}, u32[]{:S(2)}) copy-start(pred[1024]{0:T(1024)(128)(4,1)} %fusion.92) | copy-start | bytes 3076
  118.9 5.3 %copy-start.25 = (f32[1,1,1024]{2,1,0:T(1,128)S(1)}, f32[1,1,1024]{2,1,0:T(1,128)}, u32[]{:S(2)}) copy-start(f32[1,1,1024]{2,1,0:T(1,128)} %get-tuple-element.190) | copy-start | bytes 12292
  118.9 5.3 %copy-start.26 = (f32[1,1,1024]{2,1,0:T(1,128)S(1)}, f32[1,1,1024]{2,1,0:T(1,128)}, u32[]{:S(2)}) copy-start(f32[1,1,1024]{2,1,0:T(1,128)} %get-tuple-element.191) | copy-start | bytes 12292
  124.2 2.2 copy-start.11
  127.3 5.8 %copy-start.29 = (f32[1,1,1024]{2,1,0:T(1,128)S(1)}, f32[1,1,1024]{2,1,0:T(1,128)}, u32[]{:S(2)}) copy-start(f32[1,1,1024]{2,1,0:T(1,128)} %get-tuple-element.181) | copy-start | bytes 12292
  127.3 5.8 %copy-start.30 = (f32[1,1,1024]{2,1,0:T(1,128)S(1)}, f32[1,1,1024]{2,1,0:T(1,128)}, u32[]{:S(2)}) copy-start(f32[1,1,1024]{2,1,0:T(1,128)} %get-tuple-element.182) | copy-start | bytes 12292
  127.3 5.8 %copy-start.31 = (f32[1,1,1024]{2,1,0:T(1,128)S(1)}, f32[1,1,1024]{2,1,0:T(1,128)}, u32[]{:S(2)}) copy-start(f32[1,1,1024]{2,1,0:T(1,128)} %get-tuple-element.183) | copy-start | bytes 12292
  127.3 5.8 %copy-start.32 = (f32[1,1,1024]{2,1,0:T(1,128)S(1)}, f32[1,1,1024]{2,1,0:T(1,128)}, u32[]{:S(2)}) copy-start(f32[1,1,1024]{2,1,0:T(1,128)} %get-tuple-element.184) | copy-start | bytes 12292
  127.3 5.8 %copy-start.33 = (f32[1,1,1024]{2,1,0:T(1,128)S(1)}, f32[1,1,1024]{2,1,0:T(1,128)}, u32[]{:S(2)}) copy-start(f32[1,1,1024]{2,1,0:T(1,128)} %get-tuple-element.185) | copy-start | bytes 12292
  127.3 5.8 %copy-start.34 = (f32[1,1,1024]{2,1,0:T(1,128)S(1)}, f32[1,1,1024]{2,1,0:T(1,128)}, u32[]{:S(2)}) copy-start(f32[1,1,1024]{2,1,0:T(1,128)} %get-tuple-element.186) | copy-start | bytes 12292
  133.1 1.5 copy-start.12
  133.1 1.6 copy-start.7
  133.1 1.6 copy-start.35
  133.1 1.6 copy-start.36
  133.2 1.6 copy-start.37
  133.2 1.6 copy-start.42
  133.2 1.6 copy-start.43
  133.2 1.6 copy-start.44
  134.8 1.2 copy-start.6
  135.7 1.2 copy-start.9
  136.0 1.2 copy-start.8
  136.0 1.2 copy-start.27
  136.0 1.2 copy-start.28
  136.0 1.2 copy-start.38
  136.0 1.2 copy-start.39
  136.0 1.2 copy-start.40
  136.9 1.2 copy-start.23
  136.9 1.3 copy-start.24
  136.9 1.3 copy-start.46
  139.8 2.2 copy-start.13
  139.8 2.2 copy-start.14
  139.8 2.2 copy-start.15
  139.8 2.2 copy-start.16
  140.5 11.1 %collective-permute-start.1 = (bf16[3,64,1024]{2,1,0:T(8,128)(2,1)S(1)}, bf16[3,64,1024]{2,1,0:T(8,128)(2,1)S(1)}, u32[]{:S(2)}, u32[]{:S(2)}) collective-permute-start(bf16[3,64,1024]{2,1,0:T(8,128)(2,1)S(1)} %fusion.81), channel_id=1, source_target_pairs={{0,8},{8,16},{16,24},{24,32},{32,40},{40,48},{48,56},{56,64},{64,7... | collective-permute-start | bytes 1179656 | tf_op jit(solution)/shard_map/ppermute | solution.py:15
  152.8 7.1 %copy-start.50 = (f32[512]{0:T(512)S(1)}, f32[512]{0:T(512)}, u32[]{:S(2)}) copy-start(f32[512]{0:T(512)} %get-tuple-element.6) | copy-start | bytes 6148
  (8 other events, 8.6 us)
Sparse Core Ops, SparseCore 0:
  9.6 134.3 all-gather.1
  160.0 63.3 reduce-scatter.1
